TPU v7x, 128 devices: a whole 4x4x4 slice. The times are simulated.
128 devices in a mesh: sx: 8 (over z, core), sy: 8 (over x_lo, y), rep: 2 (over x_hi).
Axes of the slice: x: 4 (x_hi: 2, x_lo: 2; x = x_hi * 2 + x_lo), y: 4, z: 4, core: 2. Of those that a mesh axis runs over, the one named last changes fastest.
Arguments:
- volume: bfloat16 [2, 32, 16, 128, 256], P('rep', None, 'sx', 'sy'), may hold values from -6 to 6
- first_kernel: bfloat16 [64, 32, 3, 3, 3], replicated, may hold values from -0.21875 to 0.21875
- first_bias: float32 [64], replicated, may hold values from -3 to 3
- second_kernel: bfloat16 [128, 64, 3, 3, 3], P('sy'), may hold values from -0.15625 to 0.15625
- second_bias: float32 [128], P('sy'), may hold values from -3 to 3
- cotangent: bfloat16 [2, 128, 8, 64, 128], P('rep', 'sy', 'sx'), may hold values from -6 to 6
Outputs:
- second_out: float32 [2, 128, 8, 64, 128], P('rep', 'sy', 'sx')
- grad_first_kernel: float32 [64, 32, 3, 3, 3], replicated
- grad_first_bias: float32 [64], replicated
- grad_second_kernel: float32 [128, 64, 3, 3, 3], P('sy')
- grad_second_bias: float32 [128], P('sy')
All inputs are finite; a program needn't handle non-finite values.
Results may differ from a plain program's by a relative error of at most 0.0045.
Values may be sent and summed in bfloat16 or wider, within the bound.
A program may use at most 128 MiB of HBM per device.

v0:
```python
import math
import jax
import jax.numpy as jnp
from jax import lax
from jax.sharding import PartitionSpec as P


def padded_2(cells, sides, width):
    for axis, dim in sides:
        count = lax.axis_size(axis)
        ends = count - 1
        head = lax.slice_in_dim(cells, 0, width, axis=dim)
        tail = lax.slice_in_dim(cells, cells.shape[dim] - width, cells.shape[dim], axis=dim)
        cells = jnp.concatenate(
            [
                lax.ppermute(tail, axis, [(i, (i + 1) % count) for i in range(ends)]),
                cells,
                lax.ppermute(head, axis, [((i + 1) % count, i) for i in range(ends)]),
            ],
            axis=dim,
        )
    return cells


def convolve(padded, kernel, z_pad):
    return lax.conv_general_dilated(
        padded[None],
        kernel,
        (1, 1, 1),
        ((0, 0), (0, 0), (z_pad, z_pad)),
        dimension_numbers=("NCDHW", "OIDHW", "NCDHW"),
        preferred_element_type=jnp.float32,
    )[0]


def weight_terms(cotan, padded):
    cells_x, cells_y, cells_z = (cotan.shape[1], cotan.shape[2], cotan.shape[3])
    terms = []
    for i in range(3):
        for j in range(3):
            for k in range(3):
                piece = padded[:, i : i + cells_x, j : j + cells_y, k : k + cells_z]
                terms.append(
                    jnp.einsum("oxyz,cxyz->oc", cotan, piece, preferred_element_type=jnp.float32)
                )
    stacked = jnp.stack(terms).reshape(3, 3, 3, cotan.shape[0], padded.shape[0])
    return stacked.transpose(3, 4, 0, 1, 2)


def pool_mean(field):
    chans, cells_x, cells_y, cells_z = field.shape
    blocks = field.astype(jnp.float32).reshape(
        chans, cells_x // 2, 2, cells_y // 2, 2, cells_z // 2, 2
    )
    return jnp.mean(blocks, axis=(2, 4, 6))


def per_device(volume, first_kernel, first_bias, second_kernel, second_bias, cotangent):
    source = volume[0]
    cotan = cotangent[0]
    half_x, half_y, half_z = (source.shape[1] // 2, source.shape[2] // 2, source.shape[3] // 2)
    count = (
        lax.axis_size("rep") * lax.axis_size("sx") * lax.axis_size("sy") * half_x * half_y * half_z
    )
    scale = 1.0 / math.sqrt(count)
    rimmed = padded_2(source, (("sx", 1), ("sy", 2)), 1)
    input_pad = jnp.pad(rimmed, ((0, 0), (0, 0), (0, 0), (1, 1)))
    pre = convolve(input_pad, first_kernel, 0) + first_bias[:, None, None, None]
    act = jnp.where(pre > 0, pre, 0.3 * pre)
    pooled = pool_mean(act).astype(jnp.bfloat16)
    pooled_x = padded_2(pooled, (("sx", 1),), 1)
    gathered = lax.all_gather(pooled_x, "sy", axis=2, tiled=True)
    pooled_pad = jnp.pad(gathered, ((0, 0), (0, 0), (1, 1), (1, 1)))
    second = convolve(pooled_pad, second_kernel, 0) + second_bias[:, None, None, None]
    second_out = second.astype(jnp.float32)
    local_w2 = weight_terms(cotan, pooled_pad)
    local_b2 = jnp.sum(cotan.astype(jnp.float32), axis=(1, 2, 3))
    cot_x = padded_2(cotan, (("sx", 1),), 1)
    cot_pad = jnp.pad(cot_x, ((0, 0), (0, 0), (1, 1), (1, 1)))
    flipped = second_kernel.transpose(1, 0, 2, 3, 4)[:, :, ::-1, ::-1, ::-1]
    partial_back = convolve(cot_pad, flipped, 0)
    back = lax.psum_scatter(partial_back, "sy", scatter_dimension=2, tiled=True)
    summed_w2, summed_b2 = lax.psum((local_w2, local_b2), ("sx", "rep"))
    spread = jnp.repeat(jnp.repeat(jnp.repeat(back, 2, axis=1), 2, axis=2), 2, axis=3)
    grad_pre = (spread * 0.125 * jnp.where(pre > 0, 1.0, 0.3)).astype(jnp.bfloat16)
    local_w1 = weight_terms(grad_pre, input_pad)
    local_b1 = jnp.sum(grad_pre.astype(jnp.float32), axis=(1, 2, 3))
    summed_w1, summed_b1 = lax.psum((local_w1, local_b1), ("sx", "sy", "rep"))
    return (
        second_out[None],
        scale * summed_w1,
        scale * summed_b1,
        scale * summed_w2,
        scale * summed_b2,
    )


def solution(mesh):
    placed = (
        P("rep", None, "sx", "sy", None),
        P(),
        P(),
        P("sy", None, None, None, None),
        P("sy"),
        P("rep", "sy", "sx", None, None),
    )
    return jax.shard_map(
        per_device,
        mesh=mesh,
        in_specs=placed,
        out_specs=(
            P("rep", "sy", "sx", None, None),
            P(),
            P(),
            P("sy", None, None, None, None),
            P("sy"),
        ),
        check_vma=False,
    )
```

profile of v0, /device:TPU:1, one launch (start us, length us, event | category | flops | bytes accessed | tf_op | source)
XLA Modules:
  0.0 535.4 jit_solution(5171773666828313169)
XLA Ops:
  8.7 4.9 collective-permute-start.6
  15.5 4.2 collective-permute-done.6
  19.7 4.4 collective-permute-done.7
  25.9 6.1 %copy.331 = bf16[16,3,66,1,8,17]{0,4,5,2,1,3:T(8,128)(2,1)} copy(bf16[16,3,66,1,8,17]{2,0,5,4,1,3:T(8,128)(2,1)S(1)} %bitcast.640) | data formatting | bytes 1723392 | tf_op jit(solution)/shard_map/conv_general_dilated | solution.py:26
  33.4 9.5 %broadcast_select_fusion = f32[1,64,8,17,64]{4,2,3,1,0:T(8,128)S(1)} fusion(pred[8,17]{0,1:T(8,128)(4,1)S(1)} %copy-done.20, bf16[16,64,3,3,3]{1,0,4,3,2:T(8,128)(2,1)S(1)} %copy-done.17, bf16[16,3,66,1,7,2]{0,4,5,2,1,3:T(8,128)(2,1)S(1)} %slice.266, bf16[16,3,66,1,8,17]{0,4,5,2,1,3:T(8,128)(2,1)} %copy.331), kind=kOutput, calls=%fused_computation.70 | convolution fusion | flops 484742656 | bytes 3234056 | tf_op jit(solution)/shard_map/conv_general_dilated | solution.py:26
  52.9 4.7 collective-permute-done.1
  63.5 4.2 collective-permute-done.3
  69.6 5.4 %reshape.246 = bf16[32,4,18,1,8,33]{5,4,0,2,1,3:T(8,128)(2,1)} reshape(bf16[32,4,18,1,264]{4,0,2,1,3:T(8,128)(2,1)S(1)} %pad.15) | data formatting | bytes 2433024 | tf_op jit(solution)/shard_map/conv_general_dilated | solution.py:26
  75.0 9.3 %copy.321 = bf16[32,4,18,1,8,33]{0,4,5,2,1,3:T(8,128)(2,1)} copy(bf16[32,4,18,1,8,33]{5,4,0,2,1,3:T(8,128)(2,1)} %reshape.246) | data formatting | bytes 2433024 | tf_op jit(solution)/shard_map/conv_general_dilated | solution.py:26
  85.4 12.4 %compare_select_fusion = (f32[2,16,8,33,64]{4,2,3,1,0:T(8,128)}, f32[2,16,8,33,64]{4,2,3,1,0:T(8,128)S(1)}, f32[2,16,8,33,64]{4,2,3,1,0:T(8,128)}) fusion(f32[64]{0:T(128)S(1)} %copy-done.15, bf16[64,32,3,3,3]{0,1,4,3,2:T(8,128)(2,1)S(1)} %copy-done, bf16[32,4,18,1,7,2]{0,4,5,2,1,3:T(8,128)(2,1)S(1)} %slice.262, bf16[32,4,18,1,8,33]{0,4,5,2,1,3:T(8,128)(2,1)} %copy.321, ...), kind=kOutput, calls=%fused_computation.44 | convolution fusion | flops 941395968 | bytes 7880200 | tf_op jit(solution)/shard_map/conv_general_dilated | solution.py:26
  104.2 3.3 collective-permute-start.4
  114.9 5.1 copy.419
  120.0 5.1 copy.349
  126.7 11.1 %select_maximum_fusion = bf16[32,4,18,258]{3,0,2,1:T(8,128)(2,1)} fusion(bf16[32,4,1,256]{3,0,2,1:T(8,128)(2,1)S(1)} %collective-permute-done.3, bf16[32,4,1,256]{3,0,2,1:T(8,128)(2,1)S(1)} %collective-permute-done.2, bf16[32,1,16,256]{3,0,2,1:T(8,128)(2,1)S(1)} %collective-permute-done.1, bf16[32,2,16,256]{3,0,2,1:T(8,128)(2,1)S(1)} %bitcast.630, ...), kind=kLoop, calls=%fused_computation.77 | loop fusion | flops 10699776 | bytes 2368512 | tf_op jit(solution)/shard_map/concatenate | solution.py:14
  182.9 36.2 %psum.31 = f32[16]{0:T(128)S(1)} all-reduce(f32[16]{0:T(128)S(1)} %convert_reduce_fusion.1), channel_id=1, replica_groups=mesh['sx'=8,'sy'=8,'rep'=2] {'sx','rep'}, use_global_device_ids=true, to_apply=%region_8.9 | all-reduce | flops 16 | bytes 128 | tf_op jit(solution)/shard_map/psum | solution.py:83
  219.7 66.4 %psum.29 = f32[64]{0:T(128)S(1)} all-reduce(f32[64]{0:T(128)S(1)} %get-tuple-element.30), channel_id=1, replica_groups=mesh['sx'=8,'sy'=8,'rep'=2] {'sx','sy','rep'}, use_global_device_ids=true, to_apply=%region_5.6 | all-reduce | flops 64 | bytes 512 | tf_op jit(solution)/shard_map/psum | solution.py:88
  286.6 41.3 %all-reduce.6.cloned.1.call-done = f32[64,32,3,3,3]{0,1,4,3,2:T(8,128)} async-done(((f32[64,32,3,3,3]{0,1,4,3,2:T(8,128)}), f32[64,32,3,3,3]{0,1,4,3,2:T(8,128)}) %all-reduce.6.cloned.1.call-update) | async-done | bytes 221200 | tf_op jit(solution)/shard_map/psum | solution.py:88
  329.7 40.3 %all-gather.2.cloned.1.call-done = bf16[64,3,64,128]{3,0,2,1:T(8,128)(2,1)} async-done(((bf16[64,3,8,128]{3,0,2,1:T(8,128)(2,1)}), bf16[64,3,64,128]{3,0,2,1:T(8,128)(2,1)}) %all-gather.2.cloned.1.call-update) | async-done | bytes 3145744 | tf_op jit(solution)/shard_map/all_gather | solution.py:72
  385.5 5.5 %pad_bitcast_fusion = bf16[64,3,66,1,130]{4,0,2,1,3:T(8,128)(2,1)} fusion(bf16[64,3,64,128]{3,0,2,1:T(8,128)(2,1)S(1)} %copy-done.2), kind=kLoop, calls=%fused_computation.24 | loop fusion | bytes 6440448 | tf_op jit(solution)/shard_map/broadcast_in_dim | solution.py:27
  391.0 14.8 %copy.420 = bf16[64,3,66,1,130]{2,0,4,1,3:T(8,128)(2,1)} copy(bf16[64,3,66,1,130]{4,0,2,1,3:T(8,128)(2,1)} %pad_bitcast_fusion) | data formatting | bytes 6589440
  405.8 7.5 %pad.17.clone = bf16[64,3,66,1,136]{2,0,4,1,3:T(8,128)(2,1)} pad(bf16[64,3,66,1,130]{2,0,4,1,3:T(8,128)(2,1)} %copy.420, bf16[]{:T(256)} %constant.6.clone.1), padding=0_0x0_0x0_0x0_0x0_6 | pad | bytes 6741506 | tf_op jit(solution)/shard_map/broadcast_in_dim | solution.py:27
  413.3 11.8 %copy.326 = bf16[64,3,66,1,8,17]{0,4,5,2,1,3:T(8,128)(2,1)} copy(bf16[64,3,66,1,8,17]{2,0,5,4,1,3:T(8,128)(2,1)} %bitcast.623) | data formatting | bytes 6893568 | tf_op jit(solution)/shard_map/conv_general_dilated | solution.py:26
  426.5 19.6 %fusion.9 = f32[1,64,8,17,16]{4,2,3,1,0:T(8,128)} fusion(bf16[16,64,3,3,3]{1,0,4,3,2:T(8,128)(2,1)S(1)} %copy-done.18, bf16[64,3,66,1,7,2]{0,4,5,2,1,3:T(8,128)(2,1)S(1)} %slice.264, bf16[64,3,66,1,8,17]{0,4,5,2,1,3:T(8,128)(2,1)} %copy.326), kind=kOutput, calls=%fused_computation.36 | convolution fusion | flops 492853248 | bytes 4413952 | tf_op jit(solution)/shard_map/conv_general_dilated | solution.py:26
  450.9 75.9 %all-reduce.8.cloned.1.call-done = f32[16,64,3,3,3]{1,0,4,3,2:T(8,128)} async-done(((f32[16,64,3,3,3]{1,0,4,3,2:T(8,128)}), f32[16,64,3,3,3]{1,0,4,3,2:T(8,128)}) %all-reduce.8.cloned.1.call-update) | async-done | bytes 110608 | tf_op jit(solution)/shard_map/psum | solution.py:83
  (157 shorter events, 111.6 us)
Async XLA Ops:
  7.2 78.2 %copy-start = (bf16[64,32,3,3,3]{0,1,4,3,2:T(8,128)(2,1)S(1)}, bf16[64,32,3,3,3]{0,1,4,3,2:T(8,128)(2,1)}, u32[]{:S(2)}) copy-start(bf16[64,32,3,3,3]{0,1,4,3,2:T(8,128)(2,1)} %param.7) | copy-start | bytes 331780
  7.2 130.7 %reduce-scatter.2.cloned.1.call-start = ((), (), s32[]{:S(2)}) async-start(), calls=%async_computation.2 | async-start | bytes 4718592 | tf_op jit(solution)/shard_map/reduce_scatter | solution.py:82
  8.7 11.0 %collective-permute-start.6 = (bf16[16,1,64,128]{2,0,3,1:T(8,128)(2,1)S(1)}, bf16[16,1,64,128]{2,0,3,1:T(8,128)(2,1)S(1)}, u32[]{:S(2)}, u32[]{:S(2)}) collective-permute-start(bf16[16,1,64,128]{2,0,3,1:T(8,128)(2,1)S(1)} %bitcast.641), channel_id=1, source_target_pairs={{0,16},{16,32},{32,48},{48,64},{64,80},{80,96},{96,112},{1,17},{17... | collective-permute-start | bytes 786440 | tf_op jit(solution)/shard_map/ppermute | solution.py:16
  13.6 10.5 %collective-permute-start.7 = (bf16[16,1,64,128]{2,0,3,1:T(8,128)(2,1)S(1)}, bf16[16,1,64,128]{2,0,3,1:T(8,128)(2,1)S(1)}, u32[]{:S(2)}, u32[]{:S(2)}) collective-permute-start(bf16[16,1,64,128]{2,0,3,1:T(8,128)(2,1)S(1)} %bitcast.642), channel_id=1, source_target_pairs={{16,0},{32,16},{48,32},{64,48},{80,64},{96,80},{112,96},{17,1},{33... | collective-permute-start | bytes 786440 | tf_op jit(solution)/shard_map/ppermute | solution.py:18
  25.9 7.5 %copy-start.17 = (bf16[16,64,3,3,3]{1,0,4,3,2:T(8,128)(2,1)S(1)}, bf16[16,64,3,3,3]{1,0,4,3,2:T(8,128)(2,1)}, u32[]{:S(2)}) copy-start(bf16[16,64,3,3,3]{1,0,4,3,2:T(8,128)(2,1)} %param.9) | copy-start | bytes 165892
  25.9 7.5 %copy-start.20 = (pred[8,17]{0,1:T(8,128)(4,1)S(1)}, pred[8,17]{0,1:T(8,128)(4,1)}, u32[]{:S(2)}) copy-start(pred[8,17]{0,1:T(8,128)(4,1)} %constant.43) | copy-start | bytes 412
  46.3 281.6 %all-reduce.6.cloned.1.call-start = ((), (), s32[]{:S(2)}) async-start(), calls=%async_computation.3 | async-start | bytes 884736 | tf_op jit(solution)/shard_map/psum | solution.py:88
  47.7 5.2 collective-permute-start
  49.6 8.0 %collective-permute-start.1 = (bf16[32,1,16,256]{3,0,2,1:T(8,128)(2,1)S(1)}, bf16[32,1,16,256]{3,0,2,1:T(8,128)(2,1)S(1)}, u32[]{:S(2)}, u32[]{:S(2)}) collective-permute-start(bf16[32,1,16,256]{3,0,2,1:T(8,128)(2,1)S(1)} %get-tuple-element.39), channel_id=1, source_target_pairs={{16,0},{32,16},{48,32},{64,48},{80,64},{96,80},{112,96},{17,1},{33... | collective-permute-start | bytes 786440 | tf_op jit(solution)/shard_map/ppermute | solution.py:18
  52.9 14.9 %copy-start.4 = (bf16[32,1,16,256]{3,0,2,1:T(8,128)(2,1)}, bf16[32,1,16,256]{3,0,2,1:T(8,128)(2,1)S(1)}, u32[]{:S(2)}) copy-start(bf16[32,1,16,256]{3,0,2,1:T(8,128)(2,1)S(1)} %collective-permute-done) | copy-start | bytes 786436
  57.6 5.9 %collective-permute-start.2 = (bf16[32,4,1,256]{3,0,2,1:T(8,128)(2,1)S(1)}, bf16[32,4,1,256]{3,0,2,1:T(8,128)(2,1)S(1)}, u32[]{:S(2)}, u32[]{:S(2)}) collective-permute-start(bf16[32,4,1,256]{3,0,2,1:T(8,128)(2,1)S(1)} %get-tuple-element.36), channel_id=1, source_target_pairs={{0,2},{2,4},{4,6},{6,8},{8,10},{10,12},{12,14},{1,3},{3,5},{5,7},{... | collective-permute-start | bytes 196616 | tf_op jit(solution)/shard_map/ppermute | solution.py:16
  60.8 6.9 %collective-permute-start.3 = (bf16[32,4,1,256]{3,0,2,1:T(8,128)(2,1)S(1)}, bf16[32,4,1,256]{3,0,2,1:T(8,128)(2,1)S(1)}, u32[]{:S(2)}, u32[]{:S(2)}) collective-permute-start(bf16[32,4,1,256]{3,0,2,1:T(8,128)(2,1)S(1)} %get-tuple-element.37), channel_id=1, source_target_pairs={{2,0},{4,2},{6,4},{8,6},{10,8},{12,10},{14,12},{3,1},{5,3},{7,5},{... | collective-permute-start | bytes 196616 | tf_op jit(solution)/shard_map/ppermute | solution.py:18
  75.0 10.4 %copy-start.15 = (f32[64]{0:T(128)S(1)}, f32[64]{0:T(128)}, u32[]{:S(2)}) copy-start(f32[64]{0:T(128)} %param.8) | copy-start | bytes 772
  75.0 10.4 %copy-start.19 = (pred[8,33]{0,1:T(8,128)(4,1)S(1)}, pred[8,33]{0,1:T(8,128)(4,1)}, u32[]{:S(2)}) copy-start(pred[8,33]{0,1:T(8,128)(4,1)} %constant.41) | copy-start | bytes 796
  104.2 76.5 %collective-permute-start.4 = (bf16[64,1,8,128]{3,0,2,1:T(8,128)(2,1)}, bf16[64,1,8,128]{3,0,2,1:T(8,128)(2,1)}, u32[]{:S(2)}, u32[]{:S(2)}) collective-permute-start(bf16[64,1,8,128]{3,0,2,1:T(8,128)(2,1)} %fusion.182), channel_id=1, source_target_pairs={{0,16},{16,32},{32,48},{48,64},{64,80},{80,96},{96,112},{1,17},{17... | collective-permute-start | bytes 393224 | tf_op jit(solution)/shard_map/ppermute | solution.py:16
  107.5 73.2 %collective-permute-start.5 = (bf16[64,1,8,128]{3,0,2,1:T(8,128)(2,1)}, bf16[64,1,8,128]{3,0,2,1:T(8,128)(2,1)}, u32[]{:S(2)}, u32[]{:S(2)}) collective-permute-start(bf16[64,1,8,128]{3,0,2,1:T(8,128)(2,1)} %fusion.182), channel_id=1, source_target_pairs={{16,0},{32,16},{48,32},{64,48},{80,64},{96,80},{112,96},{17,1},{33... | collective-permute-start | bytes 393224 | tf_op jit(solution)/shard_map/ppermute | solution.py:18
  120.0 5.1 copy-start.5
  151.9 9.2 %slice-start = ((s8[4325376]{0:T(1024)(128)(4,1)}), s8[4194304]{0:T(1024)(128)(4,1)S(1)}, s32[]{:S(2)}) async-start(s8[4325376]{0:T(1024)(128)(4,1)} %bitcast.635), calls=%async_computation.5 | async-start | bytes 8388608
  156.1 5.1 slice-start.1
  177.3 192.7 %copy-start.3 = (bf16[1,16,1,64,128]{4,3,2,1,0:T(8,128)(2,1)S(1)}, bf16[1,16,1,64,128]{4,3,2,1,0:T(8,128)(2,1)}, u32[]{:S(2)}) copy-start(bf16[1,16,1,64,128]{4,3,2,1,0:T(8,128)(2,1)} %param.11) | copy-start | bytes 786436
  180.7 189.4 %all-gather.2.cloned.1.call-start = ((), (), s32[]{:S(2)}) async-start(), calls=%async_computation.1 | async-start | bytes 3538944 | tf_op jit(solution)/shard_map/all_gather | solution.py:72
  182.6 344.2 %all-reduce.8.cloned.1.call-start = ((), (), s32[]{:S(2)}) async-start(), calls=%async_computation.4 | async-start | bytes 442368 | tf_op jit(solution)/shard_map/psum | solution.py:83
  413.3 13.2 %copy-start.18 = (bf16[16,64,3,3,3]{1,0,4,3,2:T(8,128)(2,1)S(1)}, bf16[16,64,3,3,3]{1,0,4,3,2:T(8,128)(2,1)}, u32[]{:S(2)}) copy-start(bf16[16,64,3,3,3]{1,0,4,3,2:T(8,128)(2,1)} %param.9) | copy-start | bytes 165892
  446.1 82.3 %copy-start.1 = (bf16[64,32,3,3,3]{0,1,4,3,2:T(8,128)(2,1)S(1)}, bf16[64,32,3,3,3]{0,1,4,3,2:T(8,128)(2,1)}, u32[]{:S(2)}) copy-start(bf16[64,32,3,3,3]{0,1,4,3,2:T(8,128)(2,1)} %param.7) | copy-start | bytes 331780
  (11 other events, 26.2 us)
Sparse Core Ops, SparseCore 0:
  46.4 54.4 reduce-scatter.1
  180.8 147.0 all-reduce.5
  330.1 39.8 all-gather.1
  385.7 141.0 all-reduce.7
where the time goes:
time: 545 us; the launch traced here: 535 us
  waiting for transfers between devices  177 us (32%)
  blocking collectives  103 us (19%)
  local copies, waits for them, and re-layouts  97.9 us (18%)
  matrix products  90 us (17%)
  other arithmetic  31.6 us (6%)
  starting transfers between devices  21.1 us (4%)
  between operations  14.8 us (3%)
    psum x1, waiting for transfers between devices, per_device(): summed_w2, summed_b2 = lax.psum((local_w2, local_b2), ('sx', 'rep'))  75.9 us
    psum x1, blocking collectives, per_device(): summed_w1, summed_b1 = lax.psum((local_w1, local_b1), ('sx', 'sy', 'rep'))  66.4 us
    dot_general x54, matrix products, weight_terms(): jnp.einsum('oxyz,cxyz->oc', cotan, piece, preferred_element_type=jnp.floa...  48.6 us
    conv_general_dilated x11, local copies, waits for them, and re-layouts, convolve(): lax.conv_general_dilated(padded[None], kernel, (1, 1, 1), ((0, 0), (0, 0)...  45.9 us
    conv_general_dilated x3, matrix products, convolve(): lax.conv_general_dilated(padded[None], kernel, (1, 1, 1), ((0, 0), (0, 0)...  41.4 us
    psum x1, waiting for transfers between devices, per_device(): summed_w1, summed_b1 = lax.psum((local_w1, local_b1), ('sx', 'sy', 'rep'))  41.3 us
    all_gather x1, waiting for transfers between devices, per_device(): gathered = lax.all_gather(pooled_x, 'sy', axis=2, tiled=True)  40.3 us
    psum x1, blocking collectives, per_device(): summed_w2, summed_b2 = lax.psum((local_w2, local_b2), ('sx', 'rep'))  36.2 us
  transfers between devices with their start and end apart: 12, of which 9 were waited for; matrix products, arithmetic and copies ran while one was open for 33% of the time, Pallas kernels for 0%

commit v1 on v0

--- a/solution.py
+++ b/solution.py
@@ -69,7 +69,9 @@
     act = jnp.where(pre > 0, pre, 0.3 * pre)
     pooled = pool_mean(act).astype(jnp.bfloat16)
     pooled_x = padded_2(pooled, (("sx", 1),), 1)
-    gathered = lax.all_gather(pooled_x, "sy", axis=2, tiled=True)
+    gathered = jnp.concatenate(
+        lax.all_to_all(jnp.stack([pooled_x] * lax.axis_size("sy")), "sy", 0, 0), axis=2
+    )
     pooled_pad = jnp.pad(gathered, ((0, 0), (0, 0), (1, 1), (1, 1)))
     second = convolve(pooled_pad, second_kernel, 0) + second_bias[:, None, None, None]
     second_out = second.astype(jnp.float32)

time: 545 us -> 500 us (0.917)
  waiting for transfers between devices: 177 us -> 134 us
  local copies, waits for them, and re-layouts: 97.9 us -> 109 us
  other arithmetic: 31.6 us -> 21.2 us
  starting transfers between devices: 21.1 us -> 27.1 us
    psum x1, waiting for transfers between devices: 75.9 us -> 32.2 us  [per_device(): summed_w2, summed_b2 = lax.psum((local_w2, local_b2), ('sx', 'rep'))]
    all_gather x1 -> x0, waiting for transfers between devices: 40.3 us -> none  [per_device(): gathered = lax.all_gather(pooled_x, 'sy', axis=2, tiled=True)]
    psum x1, waiting for transfers between devices: 41.3 us -> 77.1 us  [per_device(): summed_w1, summed_b1 = lax.psum((local_w1, local_b1), ('sx', 'sy', 'rep'))]
    concatenate x3, other arithmetic: 14.5 us -> 4.37 us  [padded_2(): jnp.concatenate([lax.ppermute(tail, axis, [(i, (i + 1) % count) for i in...]
    all_to_all x0 -> x1, starting transfers between devices: none -> 5.83 us  [per_device(): lax.all_to_all(jnp.stack([pooled_x] * lax.axis_size('sy')), 'sy', 0, 0)]
    unnamed x51 -> x57, local copies, waits for them, and re-layouts: 25.9 us -> 27 us
  transfers between devices with their start and end apart: 12 -> 12, of which waited for: 9 -> 9; matrix products, arithmetic and copies ran while one was open for 33% -> 24% of each run, Pallas kernels for 0% -> 0%
where the time goes in v1:
time: 500 us; the launch traced here: 496 us
  waiting for transfers between devices  134 us (27%)
  local copies, waits for them, and re-layouts  109 us (22%)
  blocking collectives  99.2 us (20%)
  matrix products  88.9 us (18%)
  starting transfers between devices  27.1 us (5%)
  other arithmetic  21.2 us (4%)
  between operations  16.3 us (3%)
    psum x1, waiting for transfers between devices, per_device(): summed_w1, summed_b1 = lax.psum((local_w1, local_b1), ('sx', 'sy', 'rep'))  77.1 us
    psum x1, blocking collectives, per_device(): summed_w1, summed_b1 = lax.psum((local_w1, local_b1), ('sx', 'sy', 'rep'))  64.4 us
    conv_general_dilated x11, local copies, waits for them, and re-layouts, convolve(): lax.conv_general_dilated(padded[None], kernel, (1, 1, 1), ((0, 0), (0, 0)...  49.2 us
    dot_general x54, matrix products, weight_terms(): jnp.einsum('oxyz,cxyz->oc', cotan, piece, preferred_element_type=jnp.floa...  47 us
    conv_general_dilated x3, matrix products, convolve(): lax.conv_general_dilated(padded[None], kernel, (1, 1, 1), ((0, 0), (0, 0)...  41.9 us
    psum x1, blocking collectives, per_device(): summed_w2, summed_b2 = lax.psum((local_w2, local_b2), ('sx', 'rep'))  34.8 us
    psum x1, waiting for transfers between devices, per_device(): summed_w2, summed_b2 = lax.psum((local_w2, local_b2), ('sx', 'rep'))  32.2 us
    unnamed x57, local copies, waits for them, and re-layouts  27 us
  transfers between devices with their start and end apart: 12, of which 9 were waited for; matrix products, arithmetic and copies ran while one was open for 24% of the time, Pallas kernels for 0%

profile of v1, /device:TPU:1, one launch (start us, length us, event | category | flops | bytes accessed | tf_op | source)
XLA Modules:
  0.0 495.6 jit_solution(17816794567025119339)
XLA Ops:
  9.4 4.9 collective-permute-start
  17.7 4.4 collective-permute-done.1
  26.6 3.7 collective-permute-done.3
  32.2 5.4 %reshape.256 = bf16[32,4,18,1,8,33]{5,4,0,2,1,3:T(8,128)(2,1)} reshape(bf16[32,4,18,1,264]{4,0,2,1,3:T(8,128)(2,1)S(1)} %pad.15) | data formatting | bytes 2433024 | tf_op jit(solution)/shard_map/conv_general_dilated | solution.py:26
  37.6 9.2 %copy.324 = bf16[32,4,18,1,8,33]{0,4,5,2,1,3:T(8,128)(2,1)} copy(bf16[32,4,18,1,8,33]{5,4,0,2,1,3:T(8,128)(2,1)} %reshape.256) | data formatting | bytes 2433024 | tf_op jit(solution)/shard_map/conv_general_dilated | solution.py:26
  47.9 12.3 %compare_select_fusion = (f32[2,16,8,33,64]{4,2,3,1,0:T(8,128)}, f32[2,16,8,33,64]{4,2,3,1,0:T(8,128)S(1)}, f32[2,16,8,33,64]{4,2,3,1,0:T(8,128)}) fusion(f32[64]{0:T(128)S(1)} %copy-done.20, bf16[64,32,3,3,3]{0,1,4,3,2:T(8,128)(2,1)S(1)} %copy-done, bf16[32,4,18,1,7,2]{0,4,5,2,1,3:T(8,128)(2,1)S(1)} %slice.262, bf16[32,4,18,1,8,33]{0,4,5,2,1,3:T(8,128)(2,1)} %copy.324, ...), kind=kOutput, calls=%fused_computation.44 | convolution fusion | flops 941395968 | bytes 7880200 | tf_op jit(solution)/shard_map/conv_general_dilated | solution.py:26
  69.9 4.4 collective-permute-done.5
  77.5 5.8 %all-to-all-start = ((bf16[8,64,3,8,128]{4,1,3,2,0:T(8,128)(2,1)}), bf16[8,64,3,8,128]{4,1,3,2,0:T(8,128)(2,1)S(1)}, u32[]{:S(2)}, u32[]{:S(2)}) async-start(bf16[8,64,3,8,128]{4,1,3,2,0:T(8,128)(2,1)} %stack.179), calls=%async_computation | async-start | bytes 6291456 | tf_op jit(solution)/shard_map/all_to_all | solution.py:73
  89.1 3.9 collective-permute-done.6
  93.0 5.0 %collective-permute-done.7 = bf16[16,1,64,128]{2,0,3,1:T(8,128)(2,1)S(1)} collective-permute-done((bf16[16,1,64,128]{2,0,3,1:T(8,128)(2,1)}, bf16[16,1,64,128]{2,0,3,1:T(8,128)(2,1)S(1)}, u32[]{:S(2)}, u32[]{:S(2)}) %collective-permute-start.7) | collective-permute-done | bytes 262176 | tf_op jit(solution)/shard_map/ppermute | solution.py:18
  102.0 7.3 %copy.335 = bf16[16,3,66,1,8,17]{0,4,5,2,1,3:T(8,128)(2,1)} copy(bf16[16,3,66,1,8,17]{2,0,5,4,1,3:T(8,128)(2,1)} %bitcast.671) | data formatting | bytes 1723392 | tf_op jit(solution)/shard_map/conv_general_dilated | solution.py:26
  110.6 10.0 %broadcast_select_fusion = f32[1,64,8,17,64]{4,2,3,1,0:T(8,128)S(1)} fusion(pred[8,17]{0,1:T(8,128)(4,1)S(1)} %copy-done.23, bf16[16,64,3,3,3]{1,0,4,3,2:T(8,128)(2,1)} %param.9, bf16[16,3,66,1,7,2]{0,4,5,2,1,3:T(8,128)(2,1)S(1)} %slice.266, bf16[16,3,66,1,8,17]{0,4,5,2,1,3:T(8,128)(2,1)} %copy.335), kind=kOutput, calls=%fused_computation.70 | convolution fusion | flops 484742656 | bytes 3234056 | tf_op jit(solution)/shard_map/conv_general_dilated | solution.py:26
  142.1 4.8 slice_bitcast_fusion.1
  148.3 34.8 %psum.31 = f32[16]{0:T(128)S(1)} all-reduce(f32[16]{0:T(128)S(1)} %convert_reduce_fusion.1), channel_id=1, replica_groups=mesh['sx'=8,'sy'=8,'rep'=2] {'sx','rep'}, use_global_device_ids=true, to_apply=%region_8.9 | all-reduce | flops 16 | bytes 128 | tf_op jit(solution)/shard_map/psum | solution.py:85
  188.9 5.2 %copy.423 = f32[2,16,1,256,64]{3,1,0,4,2:T(8,128)} copy(f32[2,16,1,256,64]{4,1,3,0,2:T(8,128)} %slice.268) | data formatting | bytes 4194304
  194.1 5.2 %copy.353 = f32[2,16,8,33,64]{4,1,3,2,0:T(8,128)} copy(f32[2,16,8,33,64]{4,2,3,1,0:T(8,128)} %get-tuple-element.32) | data formatting | bytes 4325376 | tf_op jit(solution)/shard_map/jit(_where)/select_n | solution.py:87
  203.5 5.2 %pad_bitcast_fusion = bf16[64,3,66,1,130]{4,0,2,1,3:T(8,128)(2,1)} fusion(bf16[64,3,64,128]{3,0,2,1:T(8,128)(2,1)S(1)} %bitcast.625), kind=kLoop, calls=%fused_computation.24 | loop fusion | bytes 6440448 | tf_op jit(solution)/shard_map/broadcast_in_dim | solution.py:27
  208.7 14.8 %copy.424 = bf16[64,3,66,1,130]{2,0,4,1,3:T(8,128)(2,1)} copy(bf16[64,3,66,1,130]{4,0,2,1,3:T(8,128)(2,1)} %pad_bitcast_fusion) | data formatting | bytes 6589440
  223.5 7.5 %pad.17.clone = bf16[64,3,66,1,136]{2,0,4,1,3:T(8,128)(2,1)} pad(bf16[64,3,66,1,130]{2,0,4,1,3:T(8,128)(2,1)} %copy.424, bf16[]{:T(256)} %constant.6.clone.1), padding=0_0x0_0x0_0x0_0x0_6 | pad | bytes 6741506 | tf_op jit(solution)/shard_map/broadcast_in_dim | solution.py:27
  231.0 11.7 %copy.330 = bf16[64,3,66,1,8,17]{0,4,5,2,1,3:T(8,128)(2,1)} copy(bf16[64,3,66,1,8,17]{2,0,5,4,1,3:T(8,128)(2,1)} %bitcast.653) | data formatting | bytes 6893568 | tf_op jit(solution)/shard_map/conv_general_dilated | solution.py:26
  244.1 19.5 %fusion.9 = f32[1,64,8,17,16]{4,2,3,1,0:T(8,128)} fusion(bf16[16,64,3,3,3]{1,0,4,3,2:T(8,128)(2,1)S(1)} %copy-done.21, bf16[64,3,66,1,7,2]{0,4,5,2,1,3:T(8,128)(2,1)S(1)} %slice.264, bf16[64,3,66,1,8,17]{0,4,5,2,1,3:T(8,128)(2,1)} %copy.330), kind=kOutput, calls=%fused_computation.36 | convolution fusion | flops 492853248 | bytes 4413952 | tf_op jit(solution)/shard_map/conv_general_dilated | solution.py:26
  268.8 32.2 %all-reduce.8.cloned.1.call-done = f32[16,64,3,3,3]{1,0,4,3,2:T(8,128)} async-done(((f32[16,64,3,3,3]{1,0,4,3,2:T(8,128)}), f32[16,64,3,3,3]{1,0,4,3,2:T(8,128)}) %all-reduce.8.cloned.1.call-update) | async-done | bytes 110608 | tf_op jit(solution)/shard_map/psum | solution.py:85
  344.1 64.4 %psum.29 = f32[64]{0:T(128)S(1)} all-reduce(f32[64]{0:T(128)S(1)} %get-tuple-element.30), channel_id=1, replica_groups=mesh['sx'=8,'sy'=8,'rep'=2] {'sx','sy','rep'}, use_global_device_ids=true, to_apply=%region_5.6 | all-reduce | flops 64 | bytes 512 | tf_op jit(solution)/shard_map/psum | solution.py:90
  409.0 77.1 %all-reduce.6.cloned.1.call-done = f32[64,32,3,3,3]{0,1,4,3,2:T(8,128)} async-done(((f32[64,32,3,3,3]{0,1,4,3,2:T(8,128)}), f32[64,32,3,3,3]{0,1,4,3,2:T(8,128)}) %all-reduce.6.cloned.1.call-update) | async-done | bytes 221200 | tf_op jit(solution)/shard_map/psum | solution.py:90
  (164 shorter events, 120.5 us)
Async XLA Ops:
  8.0 39.9 %copy-start = (bf16[64,32,3,3,3]{0,1,4,3,2:T(8,128)(2,1)S(1)}, bf16[64,32,3,3,3]{0,1,4,3,2:T(8,128)(2,1)}, u32[]{:S(2)}) copy-start(bf16[64,32,3,3,3]{0,1,4,3,2:T(8,128)(2,1)} %param.7) | copy-start | bytes 331780
  9.4 20.9 %copy-start.3 = (bf16[1,32,2,16,256]{4,1,3,2,0:T(8,128)(2,1)}, bf16[1,32,2,16,256]{4,1,3,2,0:T(8,128)(2,1)S(1)}, u32[]{:S(2)}) copy-start(bf16[1,32,2,16,256]{4,1,3,2,0:T(8,128)(2,1)S(1)} %copy.539) | copy-start | bytes 1572868
  9.4 8.2 %collective-permute-start = (bf16[32,1,16,256]{3,0,2,1:T(8,128)(2,1)S(1)}, bf16[32,1,16,256]{3,0,2,1:T(8,128)(2,1)S(1)}, u32[]{:S(2)}, u32[]{:S(2)}) collective-permute-start(bf16[32,1,16,256]{3,0,2,1:T(8,128)(2,1)S(1)} %get-tuple-element.38), channel_id=1, source_target_pairs={{0,16},{16,32},{32,48},{48,64},{64,80},{80,96},{96,112},{1,17},{17... | collective-permute-start | bytes 786440 | tf_op jit(solution)/shard_map/ppermute | solution.py:16
  14.4 7.7 %collective-permute-start.1 = (bf16[32,1,16,256]{3,0,2,1:T(8,128)(2,1)S(1)}, bf16[32,1,16,256]{3,0,2,1:T(8,128)(2,1)S(1)}, u32[]{:S(2)}, u32[]{:S(2)}) collective-permute-start(bf16[32,1,16,256]{3,0,2,1:T(8,128)(2,1)S(1)} %get-tuple-element.39), channel_id=1, source_target_pairs={{16,0},{32,16},{48,32},{64,48},{80,64},{96,80},{112,96},{17,1},{33... | collective-permute-start | bytes 786440 | tf_op jit(solution)/shard_map/ppermute | solution.py:18
  17.7 12.6 %copy-start.9 = (bf16[32,1,16,256]{3,0,2,1:T(8,128)(2,1)}, bf16[32,1,16,256]{3,0,2,1:T(8,128)(2,1)S(1)}, u32[]{:S(2)}) copy-start(bf16[32,1,16,256]{3,0,2,1:T(8,128)(2,1)S(1)} %collective-permute-done) | copy-start | bytes 786436
  22.1 8.3 %copy-start.7 = (bf16[32,1,16,256]{3,0,2,1:T(8,128)(2,1)}, bf16[32,1,16,256]{3,0,2,1:T(8,128)(2,1)S(1)}, u32[]{:S(2)}) copy-start(bf16[32,1,16,256]{3,0,2,1:T(8,128)(2,1)S(1)} %collective-permute-done.1) | copy-start | bytes 786436
  22.1 4.5 collective-permute-start.2
  25.3 5.0 %collective-permute-start.3 = (bf16[32,4,1,256]{3,0,2,1:T(8,128)(2,1)S(1)}, bf16[32,4,1,256]{3,0,2,1:T(8,128)(2,1)S(1)}, u32[]{:S(2)}, u32[]{:S(2)}) collective-permute-start(bf16[32,4,1,256]{3,0,2,1:T(8,128)(2,1)S(1)} %get-tuple-element.37), channel_id=1, source_target_pairs={{2,0},{4,2},{6,4},{8,6},{10,8},{12,10},{14,12},{3,1},{5,3},{7,5},{... | collective-permute-start | bytes 196616 | tf_op jit(solution)/shard_map/ppermute | solution.py:18
  37.6 10.3 %copy-start.20 = (f32[64]{0:T(128)S(1)}, f32[64]{0:T(128)}, u32[]{:S(2)}) copy-start(f32[64]{0:T(128)} %param.8) | copy-start | bytes 772
  37.6 10.3 %copy-start.22 = (pred[8,33]{0,1:T(8,128)(4,1)S(1)}, pred[8,33]{0,1:T(8,128)(4,1)}, u32[]{:S(2)}) copy-start(pred[8,33]{0,1:T(8,128)(4,1)} %constant.41) | copy-start | bytes 796
  63.4 6.5 %collective-permute-start.4 = (bf16[64,1,8,128]{0,2,3,1:T(8,128)(2,1)S(1)}, bf16[64,1,8,128]{0,2,3,1:T(8,128)(2,1)S(1)}, u32[]{:S(2)}, u32[]{:S(2)}) collective-permute-start(bf16[64,1,8,128]{0,2,3,1:T(8,128)(2,1)S(1)} %fusion.182), channel_id=1, source_target_pairs={{0,16},{16,32},{32,48},{48,64},{64,80},{80,96},{96,112},{1,17},{17... | collective-permute-start | bytes 393224 | tf_op jit(solution)/shard_map/ppermute | solution.py:16
  66.6 7.7 %collective-permute-start.5 = (bf16[64,1,8,128]{0,2,3,1:T(8,128)(2,1)S(1)}, bf16[64,1,8,128]{0,2,3,1:T(8,128)(2,1)S(1)}, u32[]{:S(2)}, u32[]{:S(2)}) collective-permute-start(bf16[64,1,8,128]{0,2,3,1:T(8,128)(2,1)S(1)} %fusion.182), channel_id=1, source_target_pairs={{16,0},{32,16},{48,32},{64,48},{80,64},{96,80},{112,96},{17,1},{33... | collective-permute-start | bytes 393224 | tf_op jit(solution)/shard_map/ppermute | solution.py:18
  77.5 5.9 %copy-start.2 = (bf16[1,16,1,64,128]{4,3,2,1,0:T(8,128)(2,1)S(1)}, bf16[1,16,1,64,128]{4,3,2,1,0:T(8,128)(2,1)}, u32[]{:S(2)}) copy-start(bf16[1,16,1,64,128]{4,3,2,1,0:T(8,128)(2,1)} %param.11) | copy-start | bytes 786436
  77.5 46.1 %all-to-all-start = ((bf16[8,64,3,8,128]{4,1,3,2,0:T(8,128)(2,1)}), bf16[8,64,3,8,128]{4,1,3,2,0:T(8,128)(2,1)S(1)}, u32[]{:S(2)}, u32[]{:S(2)}) async-start(bf16[8,64,3,8,128]{4,1,3,2,0:T(8,128)(2,1)} %stack.179), calls=%async_computation | async-start | bytes 6291456 | tf_op jit(solution)/shard_map/all_to_all | solution.py:73
  83.3 217.7 %all-reduce.8.cloned.1.call-start = ((), (), s32[]{:S(2)}) async-start(), calls=%async_computation.4 | async-start | bytes 442368 | tf_op jit(solution)/shard_map/psum | solution.py:85
  84.5 8.4 %collective-permute-start.6 = (bf16[16,1,64,128]{2,0,3,1:T(8,128)(2,1)}, bf16[16,1,64,128]{2,0,3,1:T(8,128)(2,1)S(1)}, u32[]{:S(2)}, u32[]{:S(2)}) collective-permute-start(bf16[16,1,64,128]{2,0,3,1:T(8,128)(2,1)} %bitcast.672), channel_id=1, source_target_pairs={{0,16},{16,32},{32,48},{48,64},{64,80},{80,96},{96,112},{1,17},{17... | collective-permute-start | bytes 786440 | tf_op jit(solution)/shard_map/ppermute | solution.py:16
  86.8 11.2 %collective-permute-start.7 = (bf16[16,1,64,128]{2,0,3,1:T(8,128)(2,1)}, bf16[16,1,64,128]{2,0,3,1:T(8,128)(2,1)S(1)}, u32[]{:S(2)}, u32[]{:S(2)}) collective-permute-start(bf16[16,1,64,128]{2,0,3,1:T(8,128)(2,1)} %bitcast.673), channel_id=1, source_target_pairs={{16,0},{32,16},{48,32},{64,48},{80,64},{96,80},{112,96},{17,1},{33... | collective-permute-start | bytes 786440 | tf_op jit(solution)/shard_map/ppermute | solution.py:18
  102.0 8.6 %copy-start.23 = (pred[8,17]{0,1:T(8,128)(4,1)S(1)}, pred[8,17]{0,1:T(8,128)(4,1)}, u32[]{:S(2)}) copy-start(pred[8,17]{0,1:T(8,128)(4,1)} %constant.43) | copy-start | bytes 412
  141.9 160.8 %reduce-scatter.2.cloned.1.call-start = ((), (), s32[]{:S(2)}) async-start(), calls=%async_computation.2 | async-start | bytes 4718592 | tf_op jit(solution)/shard_map/reduce_scatter | solution.py:84
  146.9 339.2 %all-reduce.6.cloned.1.call-start = ((), (), s32[]{:S(2)}) async-start(), calls=%async_computation.3 | async-start | bytes 884736 | tf_op jit(solution)/shard_map/psum | solution.py:90
  194.1 5.2 %copy-start.10 = (bf16[32,1,16,256]{3,0,2,1:T(8,128)(2,1)S(1)}, bf16[32,1,16,256]{3,0,2,1:T(8,128)(2,1)}, u32[]{:S(2)}) copy-start(bf16[32,1,16,256]{3,0,2,1:T(8,128)(2,1)} %copy-done.9) | copy-start | bytes 786436
  231.0 13.1 %copy-start.21 = (bf16[16,64,3,3,3]{1,0,4,3,2:T(8,128)(2,1)S(1)}, bf16[16,64,3,3,3]{1,0,4,3,2:T(8,128)(2,1)}, u32[]{:S(2)}) copy-start(bf16[16,64,3,3,3]{1,0,4,3,2:T(8,128)(2,1)} %param.9) | copy-start | bytes 165892
  315.5 9.0 %slice-start = ((s8[4325376]{0:T(1024)(128)(4,1)}), s8[4194304]{0:T(1024)(128)(4,1)S(1)}, s32[]{:S(2)}) async-start(s8[4325376]{0:T(1024)(128)(4,1)} %bitcast.665), calls=%async_computation.5 | async-start | bytes 8388608
  339.5 148.5 %copy-start.1 = (bf16[64,32,3,3,3]{0,1,4,3,2:T(8,128)(2,1)S(1)}, bf16[64,32,3,3,3]{0,1,4,3,2:T(8,128)(2,1)}, u32[]{:S(2)}) copy-start(bf16[64,32,3,3,3]{0,1,4,3,2:T(8,128)(2,1)} %param.7) | copy-start | bytes 331780
  (14 other events, 44.0 us)
Sparse Core Ops, SparseCore 0:
  142.0 158.9 all-reduce.7
Sparse Core Ops, SparseCore 1:
  147.0 57.2 reduce-scatter.1
  344.2 141.9 all-reduce.5
